TPU v7x, 512 devices: a whole 4x8x8 slice. The times are simulated.
512 devices in a mesh: dp: 4 (over x), expert: 128 (over z, y, core).
Axes of the slice: x: 4, y: 8, z: 8, core: 2. Of those that a mesh axis runs over, the one named last changes fastest.
Arguments:
- x_rows: bfloat16 [65536, 1024], P(('dp', 'expert')), may hold values from -6 to 6
- expert_ids: int32 [65536, 1], P(('dp', 'expert')), may hold values from 0 to 127; in each aligned block of 128 rows (0 to 127, 128 to 255, ...) at most 2 rows name the same one
- gates: float32 [65536, 1], P(('dp', 'expert')), may hold values from 0.1 to 1
- cotangent: bfloat16 [65536, 1024], P(('dp', 'expert')), may hold values from -6 to 6
- w_gate: bfloat16 [128, 1024, 384], P('expert', 'dp'), may hold values from -0.1875 to 0.1875
- w_up: bfloat16 [128, 1024, 384], P('expert', 'dp'), may hold values from -0.1875 to 0.1875
- w_down: bfloat16 [128, 384, 1024], P('expert', None, 'dp'), may hold values from -0.3125 to 0.3125
Outputs:
- gated_out: bfloat16 [65536, 1024], P(('dp', 'expert'))
- input_grad: bfloat16 [65536, 1024], P(('dp', 'expert'))
- gate_grad: float32 [65536, 1], P(('dp', 'expert'))
- grad_gate: bfloat16 [128, 1024, 384], P('expert', 'dp')
- grad_up: bfloat16 [128, 1024, 384], P('expert', 'dp')
- grad_down: bfloat16 [128, 384, 1024], P('expert', None, 'dp')
Inputs may be any that keep to these rules, and one draw needn't show every extreme that they name: `expert_ids`: among the rows of one device each expert id occurs at most 2 times, and in some device's rows some expert occurs exactly 2 times.
All inputs are finite; a program needn't handle non-finite values.
Results may differ from a plain program's by a relative error of at most 0.009.
Values may be sent and summed in bfloat16 or wider, within the bound.
No kernel may reach another device: no remote copies, remote signals or barrier semaphores. Data moves between devices by JAX's collectives and lax.ppermute only.
A program may use at most 64 MiB of HBM per device.

v0:
```python
import jax
import jax.numpy as jnp
from jax import lax
from jax.sharding import PartitionSpec as P


def expert_rows(rows_in, rows_scaled, proj_gate, proj_up, proj_down):
    gate_act = jnp.dot(rows_in, proj_gate, preferred_element_type=jnp.float32)
    up_act = jnp.dot(rows_in, proj_up, preferred_element_type=jnp.float32)
    sigma = jax.nn.sigmoid(gate_act)
    hidden = (gate_act * sigma * up_act).astype(jnp.bfloat16)
    result = jnp.dot(hidden, proj_down, preferred_element_type=jnp.float32).astype(jnp.bfloat16)
    backed = jnp.dot(rows_scaled, proj_down.T, preferred_element_type=jnp.float32)
    d_gate_act = (backed * up_act * sigma * (1.0 + gate_act * (1.0 - sigma))).astype(jnp.bfloat16)
    d_up_act = (backed * gate_act * sigma).astype(jnp.bfloat16)
    d_input = (
        jnp.dot(d_gate_act, proj_gate.T, preferred_element_type=jnp.float32)
        + jnp.dot(d_up_act, proj_up.T, preferred_element_type=jnp.float32)
    ).astype(jnp.bfloat16)
    grad_g = jnp.dot(rows_in.T, d_gate_act, preferred_element_type=jnp.float32)
    grad_u = jnp.dot(rows_in.T, d_up_act, preferred_element_type=jnp.float32)
    grad_d = jnp.dot(hidden.T, rows_scaled, preferred_element_type=jnp.float32)
    return (result, d_input, (grad_g, grad_u, grad_d), (hidden, d_gate_act, d_up_act))


def per_device(x_rows, expert_ids, gates, cotangent, w_gate, w_up, w_down):
    full_gate, full_up, full_down = (
        lax.all_gather(w_gate, "dp", axis=1, tiled=True),
        lax.all_gather(w_up, "dp", axis=1, tiled=True),
        lax.all_gather(w_down, "dp", axis=2, tiled=True),
    )
    proj_gate = full_gate[0]
    proj_up = full_up[0]
    proj_down = full_down[0]
    experts = lax.axis_size("expert")
    row_count = x_rows.shape[0]
    width = x_rows.shape[1]
    capacity = 2 * row_count // experts
    row_ids = expert_ids[:, 0]
    onehot = (row_ids[:, None] == jnp.arange(experts, dtype=jnp.int32)[None, :]).astype(jnp.int32)
    ranking = jnp.sum((jnp.cumsum(onehot, 0) - onehot) * onehot, 1)
    slot = row_ids * capacity + ranking
    counts = jnp.sum(onehot, 0)
    scaled = (gates * cotangent.astype(jnp.float32)).astype(jnp.bfloat16)
    send_in = (
        jnp.zeros((experts * capacity, width), jnp.bfloat16)
        .at[slot]
        .set(x_rows)
        .reshape(experts, capacity, width)
    )
    send_scaled = (
        jnp.zeros((experts * capacity, width), jnp.bfloat16)
        .at[slot]
        .set(scaled)
        .reshape(experts, capacity, width)
    )
    recv_in, recv_scaled, recv_counts = (
        lax.all_to_all(send_in, "expert", split_axis=0, concat_axis=0, tiled=True),
        lax.all_to_all(send_scaled, "expert", split_axis=0, concat_axis=0, tiled=True),
        lax.all_to_all(
            counts.reshape(experts, 1), "expert", split_axis=0, concat_axis=0, tiled=True
        ),
    )
    flat_in = recv_in.reshape(experts * capacity, width)
    flat_scaled = recv_scaled.reshape(experts * capacity, width)
    slot_out, slot_grad, grads, acts = expert_rows(
        flat_in, flat_scaled, proj_gate, proj_up, proj_down
    )
    back_result, back_input = (
        lax.all_to_all(
            slot_out.reshape(experts, capacity, width),
            "expert",
            split_axis=0,
            concat_axis=0,
            tiled=True,
        ),
        lax.all_to_all(
            slot_grad.reshape(experts, capacity, width),
            "expert",
            split_axis=0,
            concat_axis=0,
            tiled=True,
        ),
    )
    row_out = back_result.reshape(experts * capacity, width)[slot]
    input_grad = back_input.reshape(experts * capacity, width)[slot]
    gated_out = (gates * row_out.astype(jnp.float32)).astype(jnp.bfloat16)
    gate_grad = jnp.sum(
        cotangent.astype(jnp.float32) * row_out.astype(jnp.float32), 1, keepdims=True
    )
    summed_gate, summed_up, summed_down = (
        lax.psum_scatter(
            grads[0][None].astype(jnp.bfloat16), "dp", scatter_dimension=1, tiled=True
        ).astype(jnp.float32),
        lax.psum_scatter(
            grads[1][None].astype(jnp.bfloat16), "dp", scatter_dimension=1, tiled=True
        ).astype(jnp.float32),
        lax.psum_scatter(
            grads[2][None].astype(jnp.bfloat16), "dp", scatter_dimension=2, tiled=True
        ).astype(jnp.float32),
    )
    return (
        gated_out,
        input_grad,
        gate_grad,
        summed_gate.astype(jnp.bfloat16),
        summed_up.astype(jnp.bfloat16),
        summed_down.astype(jnp.bfloat16),
    )


def solution(mesh):
    in_specs = (
        P(("dp", "expert"), None),
        P(("dp", "expert"), None),
        P(("dp", "expert"), None),
        P(("dp", "expert"), None),
        P("expert", "dp", None),
        P("expert", "dp", None),
        P("expert", None, "dp"),
    )
    out_specs = (
        P(("dp", "expert"), None),
        P(("dp", "expert"), None),
        P(("dp", "expert"), None),
        P("expert", "dp", None),
        P("expert", "dp", None),
        P("expert", None, "dp"),
    )
    return jax.shard_map(
        per_device, mesh=mesh, in_specs=in_specs, out_specs=out_specs, check_vma=False
    )
```

profile of v0, /device:TPU:8, one launch (start us, length us, event | category | flops | bytes accessed | tf_op | source)
XLA Modules:
  0.0 194.1 jit_solution(5530824760676524770)
XLA Ops:
  7.2 0.7 fusion.23
  8.1 0.8 select_reduce_fusion
  8.9 0.7 fusion.24
  9.6 1.7 scatter_custom_fusion
  11.3 1.0 reshape.40
  12.3 17.4 %all-to-all-start = ((bf16[128,2,1024]{2,1,0:T(2,128)(2,1)}), bf16[128,2,1024]{2,1,0:T(2,128)(2,1)S(1)}, u32[]{:S(2)}, u32[]{:S(2)}) async-start(bf16[128,2,1024]{2,1,0:T(2,128)(2,1)} %reshape.40), calls=%async_computation | async-start | bytes 1048576 | tf_op jit(solution)/shard_map/all_to_all | solution.py:58
  29.7 1.4 scatter_custom_fusion.1
  31.1 1.0 reshape.44
  32.1 14.0 %all_gather.9 = bf16[1,1024,384]{2,1,0:T(8,128)(2,1)S(1)} all-gather(bf16[1,256,384]{2,1,0:T(8,128)(2,1)S(1)} %copy-done.6), channel_id=1, replica_groups=mesh['dp'=4,'expert'=128] {'dp'}, dimensions={1}, use_global_device_ids=true | all-gather | bytes 983040 | tf_op jit(solution)/shard_map/all_gather | solution.py:28
  46.1 3.8 %all-to-all-done = bf16[128,2,1024]{2,1,0:T(2,128)(2,1)S(1)} async-done(((bf16[128,2,1024]{2,1,0:T(2,128)(2,1)}), bf16[128,2,1024]{2,1,0:T(2,128)(2,1)S(1)}, u32[]{:S(2)}, u32[]{:S(2)}) %all-to-all-start) | async-done | bytes 524320 | tf_op jit(solution)/shard_map/all_to_all | solution.py:58
  49.9 10.5 %all-to-all-start.2 = ((bf16[128,2,1024]{2,1,0:T(2,128)(2,1)}), bf16[128,2,1024]{2,1,0:T(2,128)(2,1)}, u32[]{:S(2)}, u32[]{:S(2)}) async-start(bf16[128,2,1024]{2,1,0:T(2,128)(2,1)} %reshape.44), calls=%async_computation.2 | async-start | bytes 1048576 | tf_op jit(solution)/shard_map/all_to_all | solution.py:59
  60.5 13.7 %all_gather.10 = bf16[1,1024,384]{2,1,0:T(8,128)(2,1)S(1)} all-gather(bf16[1,256,384]{2,1,0:T(8,128)(2,1)S(1)} %copy-done.7), channel_id=1, replica_groups=mesh['dp'=4,'expert'=128] {'dp'}, dimensions={1}, use_global_device_ids=true | all-gather | bytes 983040 | tf_op jit(solution)/shard_map/all_gather | solution.py:29
  74.2 14.3 %all_gather.11 = bf16[1,384,1024]{2,1,0:T(8,128)(2,1)S(1)} all-gather(bf16[1,384,256]{2,1,0:T(8,128)(2,1)S(1)} %copy-done.8), channel_id=1, replica_groups=mesh['dp'=4,'expert'=128] {'dp'}, dimensions={2}, use_global_device_ids=true | all-gather | bytes 983040 | tf_op jit(solution)/shard_map/all_gather | solution.py:30
  88.7 1.2 fusion.12
  89.9 1.2 fusion.8
  91.1 1.2 reshape.45
  92.3 2.4 %multiply_convert_fusion = (bf16[256,384]{1,0:T(8,128)(2,1)}, bf16[256,384]{1,0:T(8,128)(2,1)S(1)}, bf16[256,384]{1,0:T(8,128)(2,1)}) fusion(f32[256,384]{1,0:T(8,128)} %fusion.12, f32[256,384]{1,0:T(8,128)} %fusion.8, bf16[256,1024]{1,0:T(8,128)(2,1)S(1)} %reshape.45, bf16[1,384,1024]{2,1,0:T(8,128)(2,1)S(1)} %all_gather.11), kind=kOutput, calls=%fused_computation.29 | convolution fusion | flops 202899456 | bytes 2686976 | tf_op jit(solution)/shard_map/dot_general | solution.py:13
  94.7 0.7 copy-done.4
  95.4 1.3 fusion
  96.8 2.3 %fusion.1 = bf16[1,1024,384]{2,1,0:T(8,128)(2,1)} fusion(bf16[256,1024]{1,0:T(8,128)(2,1)S(1)} %reshape.41, bf16[256,384]{1,0:T(8,128)(2,1)} %get-tuple-element.6), kind=kOutput, calls=%fused_computation.10 | convolution fusion | flops 201719808 | bytes 1507328 | tf_op jit(solution)/shard_map/dot_general | solution.py:21
  99.1 1.4 convolution_convert_fusion.3
  100.5 1.0 reshape.42
  101.5 13.8 %all-to-all-start.1 = ((bf16[128,2,1024]{2,1,0:T(2,128)(2,1)}), bf16[128,2,1024]{2,1,0:T(2,128)(2,1)S(1)}, u32[]{:S(2)}, u32[]{:S(2)}) async-start(bf16[128,2,1024]{2,1,0:T(2,128)(2,1)} %reshape.42), calls=%async_computation.1 | async-start | bytes 1048576 | tf_op jit(solution)/shard_map/all_to_all | solution.py:70
  115.5 1.3 fusion.2
  118.2 1.0 reshape.46
  119.2 16.2 %all-to-all-done.1 = bf16[128,2,1024]{2,1,0:T(2,128)(2,1)S(1)} async-done(((bf16[128,2,1024]{2,1,0:T(2,128)(2,1)}), bf16[128,2,1024]{2,1,0:T(2,128)(2,1)S(1)}, u32[]{:S(2)}, u32[]{:S(2)}) %all-to-all-start.1) | async-done | bytes 524320 | tf_op jit(solution)/shard_map/all_to_all | solution.py:70
  135.4 5.8 %all-to-all-start.3 = ((bf16[128,2,1024]{2,1,0:T(2,128)(2,1)}), bf16[128,2,1024]{2,1,0:T(2,128)(2,1)S(1)}, u32[]{:S(2)}, u32[]{:S(2)}) async-start(bf16[128,2,1024]{2,1,0:T(2,128)(2,1)} %reshape.46), calls=%async_computation.3 | async-start | bytes 1048576 | tf_op jit(solution)/shard_map/all_to_all | solution.py:77
  141.4 0.9 gather_fusion
  142.3 19.1 %all-to-all-done.3 = bf16[128,2,1024]{2,1,0:T(2,128)(2,1)S(1)} async-done(((bf16[128,2,1024]{2,1,0:T(2,128)(2,1)}), bf16[128,2,1024]{2,1,0:T(2,128)(2,1)S(1)}, u32[]{:S(2)}, u32[]{:S(2)}) %all-to-all-start.3) | async-done | bytes 524320 | tf_op jit(solution)/shard_map/all_to_all | solution.py:77
  161.6 1.6 gather_fusion.1
  163.2 1.3 fusion.16
  164.5 23.1 %reduce-scatter.8.cloned.1.call-done = bf16[1,384,256]{2,1,0:T(8,128)(2,1)} async-done(((bf16[1,384,1024]{2,1,0:T(8,128)(2,1)}), bf16[1,384,256]{2,1,0:T(8,128)(2,1)}) %reduce-scatter.8.cloned.1.call-update) | async-done | bytes 196624 | tf_op jit(solution)/shard_map/reduce_scatter | solution.py:98
  (35 shorter events, 2.6 us)
Async XLA Ops:
  11.3 18.4 %copy-start = (bf16[128,1024]{1,0:T(8,128)(2,1)S(1)}, bf16[128,1024]{1,0:T(8,128)(2,1)}, u32[]{:S(2)}) copy-start(bf16[128,1024]{1,0:T(8,128)(2,1)} %param.10) | copy-start | bytes 786436
  11.3 18.4 %copy-start.9 = (f32[128,1]{0,1:T(1,128)S(1)}, f32[128,1]{0,1:T(1,128)}, u32[]{:S(2)}) copy-start(f32[128,1]{0,1:T(1,128)} %param.9) | copy-start | bytes 1540
  12.3 37.6 %all-to-all-start = ((bf16[128,2,1024]{2,1,0:T(2,128)(2,1)}), bf16[128,2,1024]{2,1,0:T(2,128)(2,1)S(1)}, u32[]{:S(2)}, u32[]{:S(2)}) async-start(bf16[128,2,1024]{2,1,0:T(2,128)(2,1)} %reshape.40), calls=%async_computation | async-start | bytes 1048576 | tf_op jit(solution)/shard_map/all_to_all | solution.py:58
  29.7 2.4 %copy-start.6 = (bf16[1,256,384]{2,1,0:T(8,128)(2,1)S(1)}, bf16[1,256,384]{2,1,0:T(8,128)(2,1)}, u32[]{:S(2)}) copy-start(bf16[1,256,384]{2,1,0:T(8,128)(2,1)} %param.11) | copy-start | bytes 589828
  32.1 28.4 %copy-start.7 = (bf16[1,256,384]{2,1,0:T(8,128)(2,1)S(1)}, bf16[1,256,384]{2,1,0:T(8,128)(2,1)}, u32[]{:S(2)}) copy-start(bf16[1,256,384]{2,1,0:T(8,128)(2,1)} %param.12) | copy-start | bytes 589828
  46.1 28.1 %copy-start.8 = (bf16[1,384,256]{2,1,0:T(8,128)(2,1)S(1)}, bf16[1,384,256]{2,1,0:T(8,128)(2,1)}, u32[]{:S(2)}) copy-start(bf16[1,384,256]{2,1,0:T(8,128)(2,1)} %param.13) | copy-start | bytes 589828
  49.9 41.2 %all-to-all-start.2 = ((bf16[128,2,1024]{2,1,0:T(2,128)(2,1)}), bf16[128,2,1024]{2,1,0:T(2,128)(2,1)}, u32[]{:S(2)}, u32[]{:S(2)}) async-start(bf16[128,2,1024]{2,1,0:T(2,128)(2,1)} %reshape.44), calls=%async_computation.2 | async-start | bytes 1048576 | tf_op jit(solution)/shard_map/all_to_all | solution.py:59
  60.4 104.1 %reduce-scatter.4.cloned.1.call-start = ((), (), s32[]{:S(2)}) async-start(), calls=%async_computation.7 | async-start | bytes 983040 | tf_op jit(solution)/shard_map/reduce_scatter | solution.py:92
  94.7 0.7 copy-start.4
  96.7 67.8 %reduce-scatter.6.cloned.1.call-start = ((), (), s32[]{:S(2)}) async-start(), calls=%async_computation.8 | async-start | bytes 983040 | tf_op jit(solution)/shard_map/reduce_scatter | solution.py:95
  100.5 15.0 %copy-start.3 = (bf16[256,384]{1,0:T(8,128)(2,1)S(1)}, bf16[256,384]{1,0:T(8,128)(2,1)}, u32[]{:S(2)}) copy-start(bf16[256,384]{1,0:T(8,128)(2,1)} %get-tuple-element.8) | copy-start | bytes 589828
  101.5 34.0 %all-to-all-start.1 = ((bf16[128,2,1024]{2,1,0:T(2,128)(2,1)}), bf16[128,2,1024]{2,1,0:T(2,128)(2,1)S(1)}, u32[]{:S(2)}, u32[]{:S(2)}) async-start(bf16[128,2,1024]{2,1,0:T(2,128)(2,1)} %reshape.42), calls=%async_computation.1 | async-start | bytes 1048576 | tf_op jit(solution)/shard_map/all_to_all | solution.py:70
  115.3 1.6 copy-start.5
  115.3 72.3 %reduce-scatter.8.cloned.1.call-start = ((), (), s32[]{:S(2)}) async-start(), calls=%async_computation.9 | async-start | bytes 983040 | tf_op jit(solution)/shard_map/reduce_scatter | solution.py:98
  116.8 0.9 copy-start.2
  135.4 26.0 %all-to-all-start.3 = ((bf16[128,2,1024]{2,1,0:T(2,128)(2,1)}), bf16[128,2,1024]{2,1,0:T(2,128)(2,1)S(1)}, u32[]{:S(2)}, u32[]{:S(2)}) async-start(bf16[128,2,1024]{2,1,0:T(2,128)(2,1)} %reshape.46), calls=%async_computation.3 | async-start | bytes 1048576 | tf_op jit(solution)/shard_map/all_to_all | solution.py:77
  161.6 1.6 copy-start.1
Sparse Core Ops, SparseCore 0:
  96.9 28.3 reduce-scatter.3
  128.7 27.6 reduce-scatter.5
  159.8 27.7 reduce-scatter.7
where the time goes:
time: 195 us; the launch traced here: 194 us
  waiting for transfers between devices  62.2 us (32%)
  starting transfers between devices  47.7 us (24%)
  blocking collectives  42 us (22%)
  between operations  14 us (7%)
  matrix products  12 us (6%)
  local copies, waits for them, and re-layouts  11.1 us (6%)
  other arithmetic  5.11 us (3%)
    reduce_scatter x1, waiting for transfers between devices, per_device(): lax.psum_scatter(grads[2][None].astype(jnp.bfloat16), 'dp', scatter_dimen...  23.1 us
    all_to_all x1, waiting for transfers between devices, per_device(): lax.all_to_all(slot_grad.reshape(experts, capacity, width), 'expert', spl...  19.1 us
    all_to_all x1, starting transfers between devices, per_device(): lax.all_to_all(send_in, 'expert', split_axis=0, concat_axis=0, tiled=True)  17.4 us
    all_to_all x1, waiting for transfers between devices, per_device(): lax.all_to_all(slot_out.reshape(experts, capacity, width), 'expert', spli...  16.2 us
    all_gather x1, blocking collectives, per_device(): lax.all_gather(w_down, 'dp', axis=2, tiled=True)  14.3 us
    all_gather x1, blocking collectives, per_device(): lax.all_gather(w_gate, 'dp', axis=1, tiled=True)  14 us
    all_to_all x1, starting transfers between devices, per_device(): lax.all_to_all(slot_out.reshape(experts, capacity, width), 'expert', spli...  13.8 us
    all_gather x1, blocking collectives, per_device(): lax.all_gather(w_up, 'dp', axis=1, tiled=True)  13.7 us
  transfers between devices with their start and end apart: 7, of which 4 were waited for; matrix products, arithmetic and copies ran while one was open for 9% of the time, Pallas kernels for 0%

commit v1 on v0

--- a/solution.py
+++ b/solution.py
@@ -25,7 +25,9 @@
 
 def per_device(x_rows, expert_ids, gates, cotangent, w_gate, w_up, w_down):
     full_gate, full_up, full_down = (
-        lax.all_gather(w_gate, "dp", axis=1, tiled=True),
+        jnp.concatenate(
+            lax.all_to_all(jnp.stack([w_gate] * lax.axis_size("dp")), "dp", 0, 0), axis=1
+        ),
         lax.all_gather(w_up, "dp", axis=1, tiled=True),
         lax.all_gather(w_down, "dp", axis=2, tiled=True),
     )

time: 195 us -> 202 us (1.036)
  waiting for transfers between devices: 62.2 us -> 84.5 us
  blocking collectives: 42 us -> 27.6 us
    all_gather x1 -> x0, blocking collectives: 14 us -> none  [per_device(): lax.all_gather(w_gate, 'dp', axis=1, tiled=True)]
    all_to_all x1, waiting for transfers between devices: 3.8 us -> 17.8 us  [per_device(): lax.all_to_all(send_in, 'expert', split_axis=0, concat_axis=0, tiled=True)]
    all_to_all x0 -> x1, waiting for transfers between devices: none -> 9.07 us  [per_device(): lax.all_to_all(jnp.stack([w_gate] * lax.axis_size('dp')), 'dp', 0, 0)]
    all_to_all x0 -> x1, starting transfers between devices: none -> 4.29 us  [per_device(): lax.all_to_all(jnp.stack([w_gate] * lax.axis_size('dp')), 'dp', 0, 0)]
    all_to_all x1, starting transfers between devices: 10.5 us -> 6.42 us  [per_device(): lax.all_to_all(send_scaled, 'expert', split_axis=0, concat_axis=0, tiled=...]
  transfers between devices with their start and end apart: 7 -> 8, of which waited for: 4 -> 5; matrix products, arithmetic and copies ran while one was open for 9% -> 10% of each run, Pallas kernels for 0% -> 0%
where the time goes in v1:
time: 202 us
  waiting for transfers between devices  84.5 us (42%)
  starting transfers between devices  47.5 us (24%)
  blocking collectives  27.6 us (14%)
  between operations  14 us (7%)
  local copies, waits for them, and re-layouts  13 us (6%)
  matrix products  12 us (6%)
  other arithmetic  3.14 us (2%)
    reduce_scatter x1, waiting for transfers between devices, per_device(): lax.psum_scatter(grads[2][None].astype(jnp.bfloat16), 'dp', scatter_dimen...  22.3 us
    all_to_all x1, waiting for transfers between devices, per_device(): lax.all_to_all(slot_grad.reshape(experts, capacity, width), 'expert', spl...  19.1 us
    all_to_all x1, waiting for transfers between devices, per_device(): lax.all_to_all(send_in, 'expert', split_axis=0, concat_axis=0, tiled=True)  17.8 us
    all_to_all x1, starting transfers between devices, per_device(): lax.all_to_all(send_in, 'expert', split_axis=0, concat_axis=0, tiled=True)  17.4 us
    all_to_all x1, waiting for transfers between devices, per_device(): lax.all_to_all(slot_out.reshape(experts, capacity, width), 'expert', spli...  16.2 us
    all_gather x1, blocking collectives, per_device(): lax.all_gather(w_down, 'dp', axis=2, tiled=True)  14.1 us
    all_gather x1, blocking collectives, per_device(): lax.all_gather(w_up, 'dp', axis=1, tiled=True)  13.5 us
    all_to_all x1, starting transfers between devices, per_device(): lax.all_to_all(slot_out.reshape(experts, capacity, width), 'expert', spli...  13.3 us
  transfers between devices with their start and end apart: 8, of which 5 were waited for; matrix products, arithmetic and copies ran while one was open for 10% of the time, Pallas kernels for 0%

profile of v1, /device:TPU:8, one launch (start us, length us, event | category | flops | bytes accessed | tf_op | source)
XLA Modules:
  0.0 201.8 jit_solution(14055251979376128768)
XLA Ops:
  7.2 1.9 stack.2
  9.1 4.3 %all-to-all-start.1 = ((bf16[4,1,256,384]{3,2,1,0:T(8,128)(2,1)}), bf16[4,1,256,384]{3,2,1,0:T(8,128)(2,1)S(1)}, u32[]{:S(2)}, u32[]{:S(2)}) async-start(bf16[4,1,256,384]{3,2,1,0:T(8,128)(2,1)} %stack.2), calls=%async_computation.1 | async-start | bytes 1572864 | tf_op jit(solution)/shard_map/all_to_all | solution.py:29
  13.8 1.7 scatter_custom_fusion
  15.6 1.0 reshape.43
  16.6 9.1 %all-to-all-done.1 = bf16[4,1,256,384]{3,2,1,0:T(8,128)(2,1)S(1)} async-done(((bf16[4,1,256,384]{3,2,1,0:T(8,128)(2,1)}), bf16[4,1,256,384]{3,2,1,0:T(8,128)(2,1)S(1)}, u32[]{:S(2)}, u32[]{:S(2)}) %all-to-all-start.1) | async-done | bytes 786464 | tf_op jit(solution)/shard_map/all_to_all | solution.py:29
  25.6 17.4 %all-to-all-start = ((bf16[128,2,1024]{2,1,0:T(2,128)(2,1)}), bf16[128,2,1024]{2,1,0:T(2,128)(2,1)S(1)}, u32[]{:S(2)}, u32[]{:S(2)}) async-start(bf16[128,2,1024]{2,1,0:T(2,128)(2,1)} %reshape.43), calls=%async_computation | async-start | bytes 1048576 | tf_op jit(solution)/shard_map/all_to_all | solution.py:60
  43.0 1.4 scatter_custom_fusion.1
  44.4 1.0 reshape.47
  45.4 17.8 %all-to-all-done = bf16[128,2,1024]{2,1,0:T(2,128)(2,1)S(1)} async-done(((bf16[128,2,1024]{2,1,0:T(2,128)(2,1)}), bf16[128,2,1024]{2,1,0:T(2,128)(2,1)S(1)}, u32[]{:S(2)}, u32[]{:S(2)}) %all-to-all-start) | async-done | bytes 524320 | tf_op jit(solution)/shard_map/all_to_all | solution.py:60
  63.2 6.4 %all-to-all-start.3 = ((bf16[128,2,1024]{2,1,0:T(2,128)(2,1)}), bf16[128,2,1024]{2,1,0:T(2,128)(2,1)}, u32[]{:S(2)}, u32[]{:S(2)}) async-start(bf16[128,2,1024]{2,1,0:T(2,128)(2,1)} %reshape.47), calls=%async_computation.3 | async-start | bytes 1048576 | tf_op jit(solution)/shard_map/all_to_all | solution.py:61
  69.7 13.5 %all_gather.6 = bf16[1,1024,384]{2,1,0:T(8,128)(2,1)S(1)} all-gather(bf16[1,256,384]{2,1,0:T(8,128)(2,1)S(1)} %copy-done.6), channel_id=1, replica_groups=mesh['dp'=4,'expert'=128] {'dp'}, dimensions={1}, use_global_device_ids=true | all-gather | bytes 983040 | tf_op jit(solution)/shard_map/all_gather | solution.py:31
  83.2 14.1 %all_gather.7 = bf16[1,384,1024]{2,1,0:T(8,128)(2,1)S(1)} all-gather(bf16[1,384,256]{2,1,0:T(8,128)(2,1)S(1)} %copy-done.7), channel_id=1, replica_groups=mesh['dp'=4,'expert'=128] {'dp'}, dimensions={2}, use_global_device_ids=true | all-gather | bytes 983040 | tf_op jit(solution)/shard_map/all_gather | solution.py:32
  97.5 1.2 fusion.21
  98.7 1.2 fusion.8
  99.9 1.2 reshape.48
  101.2 2.4 %multiply_convert_fusion = (bf16[256,384]{1,0:T(8,128)(2,1)}, bf16[256,384]{1,0:T(8,128)(2,1)S(1)}, bf16[256,384]{1,0:T(8,128)(2,1)}) fusion(f32[256,384]{1,0:T(8,128)} %fusion.21, f32[256,384]{1,0:T(8,128)} %fusion.8, bf16[256,1024]{1,0:T(8,128)(2,1)S(1)} %reshape.48, bf16[1,384,1024]{2,1,0:T(8,128)(2,1)S(1)} %all_gather.7), kind=kOutput, calls=%fused_computation.25 | convolution fusion | flops 202899456 | bytes 2686976 | tf_op jit(solution)/shard_map/dot_general | solution.py:13
  103.5 0.7 copy-done.4
  104.2 1.4 fusion
  105.6 2.3 %fusion.1 = bf16[1,1024,384]{2,1,0:T(8,128)(2,1)} fusion(bf16[256,1024]{1,0:T(8,128)(2,1)S(1)} %reshape.44, bf16[256,384]{1,0:T(8,128)(2,1)} %get-tuple-element.6), kind=kOutput, calls=%fused_computation.10 | convolution fusion | flops 201719808 | bytes 1507328 | tf_op jit(solution)/shard_map/dot_general | solution.py:21
  108.0 1.4 convolution_convert_fusion.3
  109.4 1.0 reshape.45
  110.4 13.3 %all-to-all-start.2 = ((bf16[128,2,1024]{2,1,0:T(2,128)(2,1)}), bf16[128,2,1024]{2,1,0:T(2,128)(2,1)S(1)}, u32[]{:S(2)}, u32[]{:S(2)}) async-start(bf16[128,2,1024]{2,1,0:T(2,128)(2,1)} %reshape.45), calls=%async_computation.2 | async-start | bytes 1048576 | tf_op jit(solution)/shard_map/all_to_all | solution.py:72
  124.0 1.3 fusion.2
  126.2 0.5 fusion.3
  126.7 1.0 reshape.49
  127.7 16.2 %all-to-all-done.2 = bf16[128,2,1024]{2,1,0:T(2,128)(2,1)S(1)} async-done(((bf16[128,2,1024]{2,1,0:T(2,128)(2,1)}), bf16[128,2,1024]{2,1,0:T(2,128)(2,1)S(1)}, u32[]{:S(2)}, u32[]{:S(2)}) %all-to-all-start.2) | async-done | bytes 524320 | tf_op jit(solution)/shard_map/all_to_all | solution.py:72
  143.9 5.8 %all-to-all-start.4 = ((bf16[128,2,1024]{2,1,0:T(2,128)(2,1)}), bf16[128,2,1024]{2,1,0:T(2,128)(2,1)S(1)}, u32[]{:S(2)}, u32[]{:S(2)}) async-start(bf16[128,2,1024]{2,1,0:T(2,128)(2,1)} %reshape.49), calls=%async_computation.4 | async-start | bytes 1048576 | tf_op jit(solution)/shard_map/all_to_all | solution.py:79
  149.9 0.9 gather_fusion
  150.7 19.1 %all-to-all-done.4 = bf16[128,2,1024]{2,1,0:T(2,128)(2,1)S(1)} async-done(((bf16[128,2,1024]{2,1,0:T(2,128)(2,1)}), bf16[128,2,1024]{2,1,0:T(2,128)(2,1)S(1)}, u32[]{:S(2)}, u32[]{:S(2)}) %all-to-all-start.4) | async-done | bytes 524320 | tf_op jit(solution)/shard_map/all_to_all | solution.py:79
  170.1 1.6 gather_fusion.1
  171.6 1.3 fusion.12
  173.0 22.3 %reduce-scatter.8.cloned.1.call-done = bf16[1,384,256]{2,1,0:T(8,128)(2,1)} async-done(((bf16[1,384,1024]{2,1,0:T(8,128)(2,1)}), bf16[1,384,256]{2,1,0:T(8,128)(2,1)}) %reduce-scatter.8.cloned.1.call-update) | async-done | bytes 196624 | tf_op jit(solution)/shard_map/reduce_scatter | solution.py:100
  (37 shorter events, 2.4 us)
Async XLA Ops:
  7.2 6.2 %copy-start.8 = (s32[128,1]{0,1:T(1,128)S(1)}, s32[128,1]{0,1:T(1,128)}, u32[]{:S(2)}) copy-start(s32[128,1]{0,1:T(1,128)} %param.8) | copy-start | bytes 1540
  9.1 16.6 %all-to-all-start.1 = ((bf16[4,1,256,384]{3,2,1,0:T(8,128)(2,1)}), bf16[4,1,256,384]{3,2,1,0:T(8,128)(2,1)S(1)}, u32[]{:S(2)}, u32[]{:S(2)}) async-start(bf16[4,1,256,384]{3,2,1,0:T(8,128)(2,1)} %stack.2), calls=%async_computation.1 | async-start | bytes 1572864 | tf_op jit(solution)/shard_map/all_to_all | solution.py:29
  15.5 27.5 %copy-start = (bf16[128,1024]{1,0:T(8,128)(2,1)S(1)}, bf16[128,1024]{1,0:T(8,128)(2,1)}, u32[]{:S(2)}) copy-start(bf16[128,1024]{1,0:T(8,128)(2,1)} %param.10) | copy-start | bytes 786436
  15.5 27.5 %copy-start.9 = (f32[128,1]{0,1:T(1,128)S(1)}, f32[128,1]{0,1:T(1,128)}, u32[]{:S(2)}) copy-start(f32[128,1]{0,1:T(1,128)} %param.9) | copy-start | bytes 1540
  25.6 37.6 %all-to-all-start = ((bf16[128,2,1024]{2,1,0:T(2,128)(2,1)}), bf16[128,2,1024]{2,1,0:T(2,128)(2,1)S(1)}, u32[]{:S(2)}, u32[]{:S(2)}) async-start(bf16[128,2,1024]{2,1,0:T(2,128)(2,1)} %reshape.43), calls=%async_computation | async-start | bytes 1048576 | tf_op jit(solution)/shard_map/all_to_all | solution.py:60
  44.4 25.3 %copy-start.6 = (bf16[1,256,384]{2,1,0:T(8,128)(2,1)S(1)}, bf16[1,256,384]{2,1,0:T(8,128)(2,1)}, u32[]{:S(2)}) copy-start(bf16[1,256,384]{2,1,0:T(8,128)(2,1)} %param.12) | copy-start | bytes 589828
  45.4 37.8 %copy-start.7 = (bf16[1,384,256]{2,1,0:T(8,128)(2,1)S(1)}, bf16[1,384,256]{2,1,0:T(8,128)(2,1)}, u32[]{:S(2)}) copy-start(bf16[1,384,256]{2,1,0:T(8,128)(2,1)} %param.13) | copy-start | bytes 589828
  63.2 36.7 %all-to-all-start.3 = ((bf16[128,2,1024]{2,1,0:T(2,128)(2,1)}), bf16[128,2,1024]{2,1,0:T(2,128)(2,1)}, u32[]{:S(2)}, u32[]{:S(2)}) async-start(bf16[128,2,1024]{2,1,0:T(2,128)(2,1)} %reshape.47), calls=%async_computation.3 | async-start | bytes 1048576 | tf_op jit(solution)/shard_map/all_to_all | solution.py:61
  69.6 103.3 %reduce-scatter.4.cloned.1.call-start = ((), (), s32[]{:S(2)}) async-start(), calls=%async_computation.8 | async-start | bytes 983040 | tf_op jit(solution)/shard_map/reduce_scatter | solution.py:94
  103.5 0.7 copy-start.4
  105.6 67.4 %reduce-scatter.6.cloned.1.call-start = ((), (), s32[]{:S(2)}) async-start(), calls=%async_computation.9 | async-start | bytes 983040 | tf_op jit(solution)/shard_map/reduce_scatter | solution.py:97
  109.4 14.6 %copy-start.3 = (bf16[256,384]{1,0:T(8,128)(2,1)S(1)}, bf16[256,384]{1,0:T(8,128)(2,1)}, u32[]{:S(2)}) copy-start(bf16[256,384]{1,0:T(8,128)(2,1)} %get-tuple-element.8) | copy-start | bytes 589828
  110.4 33.5 %all-to-all-start.2 = ((bf16[128,2,1024]{2,1,0:T(2,128)(2,1)}), bf16[128,2,1024]{2,1,0:T(2,128)(2,1)S(1)}, u32[]{:S(2)}, u32[]{:S(2)}) async-start(bf16[128,2,1024]{2,1,0:T(2,128)(2,1)} %reshape.45), calls=%async_computation.2 | async-start | bytes 1048576 | tf_op jit(solution)/shard_map/all_to_all | solution.py:72
  123.7 1.5 copy-start.5
  123.7 71.5 %reduce-scatter.8.cloned.1.call-start = ((), (), s32[]{:S(2)}) async-start(), calls=%async_computation.10 | async-start | bytes 983040 | tf_op jit(solution)/shard_map/reduce_scatter | solution.py:100
  125.3 0.9 copy-start.2
  143.9 26.0 %all-to-all-start.4 = ((bf16[128,2,1024]{2,1,0:T(2,128)(2,1)}), bf16[128,2,1024]{2,1,0:T(2,128)(2,1)S(1)}, u32[]{:S(2)}, u32[]{:S(2)}) async-start(bf16[128,2,1024]{2,1,0:T(2,128)(2,1)} %reshape.49), calls=%async_computation.4 | async-start | bytes 1048576 | tf_op jit(solution)/shard_map/all_to_all | solution.py:79
  170.1 1.6 copy-start.1
Sparse Core Ops, SparseCore 0:
  105.7 27.2 reduce-scatter.3
  136.4 27.5 reduce-scatter.5
  167.5 27.7 reduce-scatter.7
